TPU v7x, 32 devices: a whole 2x2x4 slice. The times are simulated.
32 devices in a mesh: lat: 2 (over y), lon: 16 (over z, x, core).
Axes of the slice: x: 2, y: 2, z: 4, core: 2. Of those that a mesh axis runs over, the one named last changes fastest.
Arguments:
- species_amounts: float32 [8, 64, 16, 128], P('lat', 'lon'), may hold values from 0.1 to 3
- thermal_anomaly: float32 [8, 64, 16], P('lat', 'lon'), may hold values from -1 to 1
- solar_flux_factor: float32 [8, 64], P('lat', 'lon'), may hold values from 0 to 1
- inner_iterations: int32 [8, 64], P('lat', 'lon'), may hold values from 4 to 36
- reference_speed: float32 [512], replicated, may hold values from 0.01 to 3
- thermal_response: float32 [512], replicated, may hold values from -1 to 1
- photo_breakup: float32 [512], replicated, may hold values from 0.03 to 3
- reaction_recipe: int32 [4, 512], replicated, may hold values from 0 to 127
- eastward_wind_ratio: float32 [16, 8, 64], P('lon', 'lat'), may hold values from -0.95 to 0.95
- northward_wind_ratio: float32 [16, 8, 64], P('lon', 'lat'), may hold values from -0.95 to 0.95
Outputs:
- transported: float32 [8, 64, 16, 128], P('lat', 'lon')
Inputs may be any that keep to these rules, and one draw needn't show every extreme that they name: `reaction_recipe`: row 0 and row 1 name the two reactants of each reaction, rows 2 and 3 its two products.
All inputs are finite; a program needn't handle non-finite values.
Results may differ from a plain program's by a relative error of at most 0.0003.
Values sent between devices are 32-bit elements; how exact they have to be, the bound alone decides.
A program may use at most 64 MiB of HBM per device.

v0:
```python
import functools
import jax
import jax.numpy as jnp
from jax import lax
from jax.experimental import pallas as pl
from jax.experimental.pallas import tpu as pltpu
from jax.sharding import PartitionSpec as P

ADV_STEPS = 2
FAST_LEAST = 1e-12
FAST_MOST = 1e8
HIGHEST = lax.Precision.HIGHEST
MOST_SUBSTEPS = 36
FLOOR = 1e-20
FLOOR_LOG = -66.43856


def with_halo(block, sides, width):
    for axis, dim in sides:
        count = lax.axis_size(axis)
        forward = [(i, i + 1) for i in range(count - 1)]
        backward = [(target, source) for source, target in forward]
        low = lax.ppermute(
            lax.slice_in_dim(block, block.shape[dim] - width, None, axis=dim), axis, forward
        )
        high = lax.ppermute(lax.slice_in_dim(block, 0, width, axis=dim), axis, backward)
        block = jnp.concatenate([low, block, high], axis=dim)
    return block


def slice_axis(array, start, count, along):
    return lax.slice_in_dim(array, start, start + count, axis=along)


def flux_sweep(padded, courant_pad, along, length):
    far_left = slice_axis(padded, 0, length + 3, along)
    near_left = slice_axis(padded, 1, length + 3, along)
    near_right = slice_axis(padded, 2, length + 3, along)
    far_right = slice_axis(padded, 3, length + 3, along)
    edges = 7.0 / 12.0 * (near_left + near_right) - 1.0 / 12.0 * (far_left + far_right)
    edges = jnp.minimum(
        jnp.maximum(edges, jnp.minimum(near_left, near_right)), jnp.maximum(near_left, near_right)
    )
    cell_means = slice_axis(padded, 2, length + 2, along)
    left_edge = slice_axis(edges, 0, length + 2, along)
    right_edge = slice_axis(edges, 1, length + 2, along)
    edge_jump = right_edge - left_edge
    curvature = 6.0 * cell_means - 3.0 * (left_edge + right_edge)
    courant = slice_axis(courant_pad, 3, length + 1, along)
    magnitude = jnp.abs(courant)
    from_left = slice_axis(right_edge, 0, length + 1, along) - 0.5 * courant * (
        slice_axis(edge_jump, 0, length + 1, along)
        - (1.0 - 2.0 / 3.0 * courant) * slice_axis(curvature, 0, length + 1, along)
    )
    from_right = slice_axis(left_edge, 1, length + 1, along) + 0.5 * magnitude * (
        slice_axis(edge_jump, 1, length + 1, along)
        + (1.0 - 2.0 / 3.0 * magnitude) * slice_axis(curvature, 1, length + 1, along)
    )
    face_flux = courant * jnp.where(courant >= 0.0, from_left, from_right)
    interior = slice_axis(padded, 3, length, along)
    return interior - (
        slice_axis(face_flux, 1, length, along) - slice_axis(face_flux, 0, length, along)
    )


def wrap_pad(array, along):
    extent = array.shape[along]
    return jnp.concatenate(
        [slice_axis(array, extent - 3, 3, along), array, slice_axis(array, 0, 3, along)], axis=along
    )


def two_halves(values):
    high = values.astype(jnp.bfloat16)
    low = (values - high.astype(jnp.float32)).astype(jnp.bfloat16)
    return jnp.concatenate([high, low], axis=1)


def dot32(left, right, dims=((1,), (0,)), precision=None):
    return lax.dot_general(
        left, right, (dims, ((), ())), precision=precision, preferred_element_type=jnp.float32
    )


def chem_kernel(*refs):
    sources, (out, rates, pick, spread, state, least, most, warmth) = refs[:8], refs[8:16]
    amounts, anomaly, solar, counts, speed, response, photo, recipe = held = refs[16:24]
    copies = [
        pltpu.make_async_copy(source, here, refs[24].at[index])
        for index, (source, here) in enumerate(zip(sources, held))
    ]
    for copy in copies:
        copy.start()
    for copy in copies:
        copy.wait()
    rows, columns, levels = anomaly.shape
    cells, species = state.shape
    width = rows * columns
    chunks = rates.shape[0]
    for row in range(rows):
        warmth[row * columns : (row + 1) * columns, :] = anomaly[row]
    place = lax.broadcasted_iota(jnp.int32, (width, species), 0)
    sunlight = jnp.zeros((width, species), jnp.float32)
    count = jnp.zeros((width, species), jnp.int32)
    longest = jnp.int32(0)
    for column in range(width):
        here = place == column
        spot = (column // columns, column % columns)
        sunlight = jnp.where(here, solar[spot], sunlight)
        count = jnp.where(here, counts[spot], count)
        longest = jnp.maximum(longest, counts[spot])
    ids = lax.broadcasted_iota(jnp.int32, (species, species), 0)
    for chunk in range(chunks):
        part = pl.ds(chunk * species, species)
        hits = [
            (recipe[row : row + 1, part] == ids).astype(jnp.float32) for row in range(4)
        ]
        taking = jnp.concatenate([hits[0], hits[1]], axis=1).astype(jnp.bfloat16)
        pick[chunk] = jnp.concatenate([taking, taking], axis=0)
        giving = jnp.concatenate(
            [jnp.transpose(hits[2] + hits[3]), jnp.transpose(hits[0] + hits[1])], axis=1
        ).astype(jnp.bfloat16)
        spread[chunk] = jnp.concatenate([giving, giving], axis=0)
    for level in range(levels):
        block = pl.ds(level * width, width)
        heat = jnp.broadcast_to(warmth[:, level : level + 1], (width, species))
        for chunk in range(chunks):
            part = pl.ds(chunk * species, species)
            rates[chunk, block, :] = (
                speed[:, part] * jnp.exp(response[:, part] * heat) + photo[:, part] * sunlight
            )

    def start():
        for level in range(levels):
            state[pl.ds(level * width, width), :] = amounts[pl.ds(level, width, stride=levels), :]

    def tiled(values):
        return jnp.concatenate([values] * levels, axis=0)

    start()
    substep = 1.0 / count.astype(jnp.float32)
    least[...] = state[...]
    most[...] = state[...]

    def advance(step, carry):
        current = state[...]
        least[...] = jnp.minimum(least[...], current)
        most[...] = jnp.maximum(most[...], current)
        pair = two_halves(current)
        flows = []
        for chunk in range(chunks):
            taken = dot32(pair, pick[chunk])
            flows.append(two_halves(rates[chunk] * taken[:, :species] * taken[:, species:]))
        total = dot32(jnp.concatenate(flows, axis=1), spread[...].reshape(-1, 2 * species))
        produced = total[:, :species]
        consumed = total[:, species:]
        size = tiled(substep)
        updated = (current + size * produced) / (current + size * consumed) * current
        state[...] = jnp.where(tiled(count) > step, updated, current)
        return carry

    lax.fori_loop(0, longest, advance, 0)
    usual = (jnp.min(least[...]) >= FAST_LEAST) & (jnp.max(most[...]) <= FAST_MOST)

    @pl.when(jnp.logical_not(usual))
    def _():
        start()

        def advance_fully(step, carry):
            current = state[...]
            produced = jnp.zeros((cells, species), jnp.float32)
            lost = jnp.zeros((cells, species), jnp.float32)
            for chunk in range(chunks):
                first_hit = pick[chunk, :species, :species].astype(jnp.float32)
                second_hit = pick[chunk, :species, species:].astype(jnp.float32)
                making = spread[chunk, :species, :species].astype(jnp.float32)
                first = dot32(current, first_hit, precision=HIGHEST)
                second = dot32(current, second_hit, precision=HIGHEST)
                rate = rates[chunk]
                produced += dot32(rate * first * second, making, precision=HIGHEST)
                lost += dot32(rate * second, first_hit, ((1,), (1,)), HIGHEST)
                lost += dot32(rate * first, second_hit, ((1,), (1,)), HIGHEST)
            size = tiled(substep)
            updated = (current + size * produced) / (1.0 + size * lost)
            state[...] = jnp.where(tiled(count) > step, updated, current)
            return carry

        lax.fori_loop(0, longest, advance_fully, 0)

    for level in range(levels):
        out[pl.ds(level, width, stride=levels), :] = state[pl.ds(level * width, width), :]


def react(operands):
    cells, species = operands[0].shape
    rows, columns, levels = operands[1].shape
    chunks = operands[7].shape[1] // species
    in_vmem = pl.BlockSpec(memory_space=pltpu.VMEM)
    held = [
        (pltpu.SMEM if index in (2, 3) else pltpu.VMEM)(operand.shape, operand.dtype)
        for index, operand in enumerate(operands)
    ]
    table = pltpu.VMEM((chunks, 2 * species, 2 * species), jnp.bfloat16)
    field = pltpu.VMEM((cells, species), jnp.float32)
    return pl.pallas_call(
        chem_kernel,
        out_shape=jax.ShapeDtypeStruct((cells, species), jnp.float32),
        in_specs=[pl.BlockSpec(memory_space=pltpu.HBM)] * len(operands),
        out_specs=in_vmem,
        scratch_shapes=[
            pltpu.VMEM((chunks, cells, species), jnp.float32), table, table,
            field, field, field, pltpu.VMEM((rows * columns, levels), jnp.float32),
            *held, pltpu.SemaphoreType.DMA((len(operands),)),
        ],
        compiler_params=pltpu.CompilerParams(vmem_limit_bytes=67043328),
    )(*operands)


def others(bands, devices):
    return [(dy, dl) for dl in range(devices) for dy in range(bands) if (dy, dl) != (0, 0)]


def peer(bands, devices, dy, dl):
    band, block = lax.axis_index("lat"), lax.axis_index("lon")
    return (lax.rem(band + dy, bands), lax.rem(block + dl, devices))


def signal_peers(bands, devices):
    barrier = pltpu.get_barrier_semaphore()
    for dy, dl in others(bands, devices):
        pl.semaphore_signal(
            barrier, inc=1, device_id=peer(bands, devices, dy, dl),
            device_id_type=pl.DeviceIdType.MESH,
        )


def wrap_rows(buffer, slot, values, half):
    extent = values.shape[0]
    buffer[slot, 8 : 8 + extent, :] = values
    buffer[slot, 0:8, :] = pltpu.roll(values[extent - 8 :], half, 1)
    buffer[slot, 8 + extent : 16 + extent, :] = pltpu.roll(values[:8], half, 1)


def clipped_edge(far_left, near_left, near_right, far_right):
    edge = 7.0 / 12.0 * (near_left + near_right) - 1.0 / 12.0 * (far_left + far_right)
    return jnp.minimum(
        jnp.maximum(edge, jnp.minimum(near_left, near_right)), jnp.maximum(near_left, near_right)
    )


def face_flow(courant, before, edge, after, left_mean, right_mean):
    magnitude = jnp.abs(courant)
    rightward = courant >= 0.0
    other = jnp.where(rightward, before, after)
    mean = jnp.where(rightward, left_mean, right_mean)
    bend = 6.0 * mean - 3.0 * (other + edge)
    return courant * (
        edge + 0.5 * magnitude * ((other - edge) + (1.0 - 2.0 / 3.0 * magnitude) * bend)
    )


def move_kernel(
    bands, devices, packed, east, north, out,
    inbox, outbox, back, wind_out, wind_in, courants, grid, edges,
    send_there, recv_there, send_wind, recv_wind, send_back, recv_back,
):
    band, block = lax.axis_index("lat"), lax.axis_index("lon")
    _, rows, longitudes = east.shape
    levels, _, _, species = packed.shape
    half = species // 2
    columns = longitudes // devices
    extent = longitudes // 2
    lats = bands * rows
    low_rows = rows // 2
    offsets = others(bands, devices)

    def remote(source, target, send_sem, recv_sem, device):
        return pltpu.make_async_remote_copy(
            src_ref=source, dst_ref=target, send_sem=send_sem, recv_sem=recv_sem,
            device_id=device, device_id_type=pl.DeviceIdType.MESH,
        )

    wind_out[...] = jnp.zeros_like(wind_out)
    wind_out[0:rows, 0:longitudes] = east[0]
    wind_out[rows : 2 * rows, 0:longitudes] = north[0]
    wind_in[band] = wind_out[...]
    inbox[band, block] = packed[block, band]
    pl.semaphore_wait(pltpu.get_barrier_semaphore(), len(offsets))

    winds = []
    for dy in range(1, bands):
        copy = remote(
            wind_out, wind_in.at[band], send_wind.at[dy], recv_wind.at[dy],
            peer(bands, devices, dy, 0),
        )
        copy.start()
        winds.append(copy)
    moves = []
    for index, (dy, dl) in enumerate(offsets):
        device = peer(bands, devices, dy, dl)
        copy = remote(
            packed.at[device[1], device[0]], inbox.at[band, block],
            send_there.at[index], recv_there.at[index], device,
        )
        copy.start()
        moves.append(copy)

    for copy in winds:
        copy.wait()
    near_tall = lax.broadcasted_iota(jnp.int32, (extent, species), 1) < half
    wide = wind_out.shape[1]
    tall = [wind_in[y] for y in range(bands)]
    tall.append(jnp.zeros((wide - bands * 2 * rows, wide), jnp.float32))
    turned = jnp.transpose(jnp.concatenate(tall, axis=0))
    for lat in range(lats):
        for kind in range(2):
            lane = lat // rows * 2 * rows + kind * rows + lat % rows
            courants[kind, lat] = jnp.where(
                near_tall,
                jnp.broadcast_to(turned[0:extent, lane : lane + 1], (extent, species)),
                jnp.broadcast_to(turned[extent : 2 * extent, lane : lane + 1], (extent, species)),
            )
    for copy in moves:
        copy.wait()

    near = lax.broadcasted_iota(jnp.int32, (low_rows * columns, species), 1) < half

    def swap_pair(first, second):
        return (
            jnp.where(near, first, pltpu.roll(second, half, 1)),
            jnp.where(near, pltpu.roll(first, half, 1), second),
        )

    for y in range(bands):
        for spot in range(devices // 2):
            pair = swap_pair(inbox[y, spot], inbox[y, spot + devices // 2])
            for high in range(2):
                for low in range(low_rows):
                    lat = y * rows + high * low_rows + low
                    grid[lat, 8 + spot * columns : 8 + (spot + 1) * columns, :] = pair[high][
                        low * columns : (low + 1) * columns
                    ]
    planes = [grid[lat, 8 : 8 + extent, :] for lat in range(lats)]
    empty = jnp.zeros((extent, species), jnp.float32)
    for sweep_index in range(ADV_STEPS):
        swept = []
        for lat in range(lats):
            mean = planes[lat]
            wrap_rows(grid, lat, mean, half)

            def shifted(buffer, shift):
                return buffer[lat, 8 + shift : 8 + shift + extent, :]

            left_mean = shifted(grid, -1)
            edge = clipped_edge(shifted(grid, -2), left_mean, mean, shifted(grid, 1))
            wrap_rows(edges, lat, edge, half)
            flow = face_flow(
                courants[0, lat], shifted(edges, -1), edge, shifted(edges, 1), left_mean, mean
            )
            wrap_rows(grid, lat, flow, half)
            swept.append(mean - (shifted(grid, 1) - flow))
        padded = [empty, empty] + swept + [empty, empty]
        rims = [clipped_edge(*padded[lat : lat + 4]) for lat in range(lats + 1)]
        flows = [
            face_flow(
                courants[1, lat], rims[lat - 1], rims[lat], rims[lat + 1],
                swept[lat - 1], swept[lat],
            )
            for lat in range(1, lats)
        ]
        flows = [empty] + flows + [empty]
        planes = [swept[lat] - (flows[lat + 1] - flows[lat]) for lat in range(lats)]
    for lat in range(lats):
        grid[lat, 8 : 8 + extent, :] = planes[lat]
    for y in range(bands):
        for spot in range(devices // 2):
            sides = [
                jnp.concatenate(
                    [
                        grid[
                            y * rows + high * low_rows + low,
                            8 + spot * columns : 8 + (spot + 1) * columns,
                            :,
                        ]
                        for low in range(low_rows)
                    ],
                    axis=0,
                )
                for high in range(2)
            ]
            outbox[y, spot], outbox[y, spot + devices // 2] = swap_pair(*sides)
    back[block, band] = outbox[band, block]
    moves = []
    for index, (dy, dl) in enumerate(offsets):
        device = peer(bands, devices, dy, dl)
        copy = remote(
            outbox.at[device[0], device[1]], back.at[block, band],
            send_back.at[index], recv_back.at[index], device,
        )
        copy.start()
        moves.append(copy)
    for copy in moves:
        copy.wait()
    count = low_rows * columns
    for level in range(levels):
        front, behind = swap_pair(back[level, 0], back[level, 1])
        out[pl.ds(level, count, stride=levels), :] = front
        out[pl.ds(count * levels + level, count, stride=levels), :] = behind


def halves(values):
    high = values.astype(jnp.bfloat16)
    return high, (values - high.astype(jnp.float32)).astype(jnp.bfloat16)


def substeps(groups, state, number, log_rates, pick, spread, *results):
    sides = range(2)
    gathered = [results[side * groups : (side + 1) * groups] for side in sides]
    scattered = [results[(2 + side) * groups : (3 + side) * groups] for side in sides]
    tall = state.shape[0] // groups
    species = state.shape[1]

    def load_pick():
        for side in sides:
            pltpu.matmul_push_rhs(pick[side], 0, side)

    def load_spread():
        for side in sides:
            pltpu.matmul_push_rhs(spread[side], 1, side)

    def gather(group, logs):
        pair = jnp.concatenate(halves(jnp.maximum(logs, FLOOR_LOG)), axis=1)
        for side in sides:
            pltpu.matmul_acc_lhs(
                gathered[side][group], pair, load_staged_rhs=None if group else 0
            )

    load_pick()
    for group in range(groups):
        gather(group, jnp.log2(state[group * tall : (group + 1) * tall, :]))
    load_spread()

    def advance(step, carry):
        for group in range(groups):
            block = slice(group * tall, (group + 1) * tall)
            for side in sides:
                logs = pltpu.matmul_pop(gathered[side][group]) + log_rates[side, block, :]
                high, low = halves(jnp.exp2(logs))
                pltpu.matmul_acc_lhs(
                    scattered[side][group], high, load_staged_rhs=None if group else 1
                )
                pltpu.matmul_acc_lhs(scattered[side][group], low)
        load_pick()
        load_spread()
        for group in range(groups):
            block = slice(group * tall, (group + 1) * tall)
            total = pltpu.matmul_pop(scattered[0][group]) + pltpu.matmul_pop(scattered[1][group])
            current, count = state[block, :], number[block, :]
            above = count * current + total[:, :species]
            below = count + total[:, species:] * (1.0 / jnp.maximum(current, FLOOR))
            gather(group, jnp.log2(above) - jnp.log2(below))
            state[block, :] = jnp.where(count > step.astype(jnp.float32), above / below, current)
        return carry

    lax.fori_loop(0, MOST_SUBSTEPS, advance, 0)
    for side in sides:
        for group in range(groups):
            pltpu.matmul_pop(gathered[side][group])
        pltpu.matmul_acc_lhs(
            scattered[side][0], jnp.zeros((tall, 2 * species), jnp.bfloat16), load_staged_rhs=1
        )
        pltpu.matmul_pop(scattered[side][0])


def whole_kernel(bands, devices, *refs):
    sources, out = refs[:10], refs[10]
    amounts, anomaly, solar, counts, speed, response, photo, recipe, east, north = held = refs[11:21]
    log_rates, pick, spread, state, number, warmth, arrived, packed = refs[21:29]
    move_refs = refs[29:]
    width = warmth.shape[0]
    cells, species = state.shape
    levels = cells // width

    signal_peers(bands, devices)
    copies = [
        pltpu.make_async_copy(source, here, arrived.at[index])
        for index, (source, here) in enumerate(zip(sources, held))
    ]
    for copy in copies:
        copy.start()
    for copy in copies:
        copy.wait()
    rows, columns, _ = anomaly.shape
    for row in range(rows):
        warmth[row * columns : (row + 1) * columns, :] = anomaly[row]
    place = lax.broadcasted_iota(jnp.int32, (width, species), 0)
    sunlight = jnp.zeros((width, species), jnp.float32)
    count = jnp.zeros((width, species), jnp.int32)
    for column in range(width):
        here = place == column
        spot = (column // columns, column % columns)
        sunlight = jnp.where(here, solar[spot], sunlight)
        count = jnp.where(here, counts[spot], count)
    count = count.astype(jnp.float32)
    ids = lax.broadcasted_iota(jnp.int32, (species, species), 0)
    for chunk in range(4):
        part = pl.ds(chunk * species, species)
        hits = [(recipe[row : row + 1, part] == ids).astype(jnp.float32) for row in range(4)]
        taking, giving = hits[0] + hits[1], hits[2] + hits[3]
        side, spot = chunk // 2, chunk % 2 * species
        for copy in range(2):
            pick[side, copy * species : (copy + 1) * species, spot : spot + species] = (
                taking.astype(jnp.bfloat16)
            )
        spread[side, spot : spot + species, :] = jnp.concatenate(
            [jnp.transpose(giving), jnp.transpose(taking)], axis=1
        ).astype(jnp.bfloat16)
    for level in range(levels):
        block = pl.ds(level * width, width)
        heat = jnp.broadcast_to(warmth[:, level : level + 1], (width, species))
        for chunk in range(4):
            part = pl.ds(chunk * species, species)
            log_rates[chunk // 2, block, chunk % 2 * species : (chunk % 2 + 1) * species] = jnp.log2(
                speed[:, part] * jnp.exp(response[:, part] * heat) + photo[:, part] * sunlight
            )
        state[block, :] = amounts[pl.ds(level, width, stride=levels), :]
        number[block, :] = count

    groups = cells // 32
    pl.run_scoped(
        functools.partial(substeps, groups, state, number, log_rates, pick, spread),
        *[
            pltpu.ACC(side)((32, 2 * species), jnp.float32)
            for use in range(2)
            for side in range(2)
            for group in range(groups)
        ],
    )

    half = species // 2
    near = lax.broadcasted_iota(jnp.int32, (width // 2, species), 1) < half
    for level in range(levels):
        front = state[pl.ds(level * width, width // 2), :]
        behind = state[pl.ds(level * width + width // 2, width // 2), :]
        packed[level, 0] = jnp.where(near, front, pltpu.roll(behind, half, 1))
        packed[level, 1] = jnp.where(near, pltpu.roll(front, half, 1), behind)
    move_kernel(bands, devices, packed, east, north, out, *move_refs)


def react_and_advect(operands):
    bands, devices = lax.axis_size("lat"), lax.axis_size("lon")
    cells, species = operands[0].shape
    rows, columns, levels = operands[1].shape
    longitudes = operands[8].shape[2]
    lats, extent, count = bands * rows, longitudes // 2, rows * columns // 2
    wide = -(-longitudes // 128) * 128
    held = [
        (pltpu.SMEM if index in (2, 3) else pltpu.VMEM)(operand.shape, operand.dtype)
        for index, operand in enumerate(operands)
    ]
    semaphores = pltpu.SemaphoreType.DMA((bands * devices - 1,))
    wind_semaphores = pltpu.SemaphoreType.DMA((bands,))
    box = pltpu.VMEM((bands, devices, count, species), jnp.float32)
    exchanged = pltpu.VMEM((levels, bands, count, species), jnp.float32)
    wrapped = pltpu.VMEM((lats, extent + 16, species), jnp.float32)
    table = pltpu.VMEM((2, 2 * species, 2 * species), jnp.bfloat16)
    field = pltpu.VMEM((cells, species), jnp.float32)
    return pl.pallas_call(
        functools.partial(whole_kernel, bands, devices),
        out_shape=jax.ShapeDtypeStruct((cells, species), jnp.float32),
        in_specs=[pl.BlockSpec(memory_space=pltpu.HBM)] * len(operands),
        out_specs=pl.BlockSpec(memory_space=pltpu.VMEM),
        scratch_shapes=[
            *held,
            pltpu.VMEM((2, cells, 2 * species), jnp.float32), table, table, field, field,
            pltpu.VMEM((rows * columns, levels), jnp.float32),
            pltpu.SemaphoreType.DMA((len(operands),)), exchanged,
            box, box, exchanged,
            pltpu.VMEM((2 * rows, wide), jnp.float32),
            pltpu.VMEM((bands, 2 * rows, wide), jnp.float32),
            pltpu.VMEM((2, lats, extent, species), jnp.float32), wrapped, wrapped,
            semaphores, semaphores, wind_semaphores, wind_semaphores, semaphores, semaphores,
        ],
        compiler_params=pltpu.CompilerParams(
            collective_id=0, has_side_effects=True, vmem_limit_bytes=32 << 20
        ),
    )(*operands)


def per_device(
    species_amounts,
    thermal_anomaly,
    solar_flux_factor,
    inner_iterations,
    reference_speed,
    thermal_response,
    photo_breakup,
    reaction_recipe,
    eastward_wind_ratio,
    northward_wind_ratio,
):
    rows, columns, levels, species = species_amounts.shape
    devices = lax.axis_size("lon")
    longitudes = eastward_wind_ratio.shape[2]
    reactions = reaction_recipe.shape[1]
    operands = (
        species_amounts.reshape(-1, species), thermal_anomaly, solar_flux_factor,
        inner_iterations, reference_speed.reshape(1, -1), thermal_response.reshape(1, -1),
        photo_breakup.reshape(1, -1), reaction_recipe,
    )
    paired = lax.axis_size("lat") == 2 and levels == devices and rows % 2 == 0
    tabled = species == 128 and reactions == 4 * species and rows * columns % 16 == 0
    if paired and tabled and devices % 2 == 0 and longitudes <= 128:
        moved = react_and_advect((*operands, eastward_wind_ratio, northward_wind_ratio))
        return moved.reshape(species_amounts.shape)
    settled_columns = react(operands).reshape(species_amounts.shape)
    lat_rows = species_amounts.shape[0]
    row_ids = lax.axis_index("lat") * lat_rows + lax.broadcasted_iota(
        jnp.int32, (lat_rows, 1, 1, 1), 0
    )
    carried_quantity = lax.all_to_all(
        settled_columns, "lon", split_axis=2, concat_axis=1, tiled=True
    )
    east_faces = jnp.transpose(eastward_wind_ratio, (1, 2, 0))[..., None]
    south_faces = jnp.where(
        row_ids > 0, jnp.transpose(northward_wind_ratio, (1, 2, 0))[..., None], 0.0
    )
    east_pad = wrap_pad(east_faces, 1)
    for sweep_index in range(ADV_STEPS):
        carried_quantity = flux_sweep(
            wrap_pad(carried_quantity, 1), east_pad, 1, carried_quantity.shape[1]
        )
        rimmed, south_pad = (
            with_halo(carried_quantity, (("lat", 0),), 3),
            with_halo(south_faces, (("lat", 0),), 3),
        )
        carried_quantity = flux_sweep(rimmed, south_pad, 0, lat_rows)
    return lax.all_to_all(carried_quantity, "lon", split_axis=1, concat_axis=2, tiled=True)


def solution(mesh):
    return jax.shard_map(
        per_device,
        mesh=mesh,
        in_specs=(
            P("lat", "lon", None, None),
            P("lat", "lon", None),
            P("lat", "lon"),
            P("lat", "lon"),
            P(),
            P(),
            P(),
            P(),
            P("lon", "lat", None),
            P("lon", "lat", None),
        ),
        out_specs=P("lat", "lon", None, None),
        check_vma=False,
    )
```

profile of v0, /device:TPU:0, one launch (start us, length us, event | category | flops | bytes accessed | tf_op | source)
XLA Modules:
  0.0 35.4 jit_solution(2807457301304193477)
XLA Ops:
  0.0 0.0 copy-start.5
  0.0 0.0 copy-start.4
  0.0 0.0 copy-start.3
  0.0 0.7 %copy-done.5 = f32[512]{0:T(512)S(1)} copy-done((f32[512]{0:T(512)S(1)}, f32[512]{0:T(512)}, u32[]{:S(2)}) %copy-start.5) | copy-done | bytes 2072
  0.7 0.0 copy-done.4
  0.7 0.0 copy-done.3
  0.7 0.0 copy-start
  0.7 0.9 %copy-done = f32[4,4,16,128]{3,2,1,0:T(8,128)S(1)} copy-done((f32[4,4,16,128]{3,2,1,0:T(8,128)S(1)}, f32[4,4,16,128]{3,2,1,0:T(8,128)}, u32[]{:S(2)}) %copy-start) | copy-done | bytes 131096
  1.6 0.0 copy-start.1
  1.6 0.7 %copy-done.1 = f32[4,4,16]{2,1,0:T(4,128)S(1)} copy-done((f32[4,4,16]{2,1,0:T(4,128)S(1)}, f32[4,4,16]{2,1,0:T(4,128)}, u32[]{:S(2)}) %copy-start.1) | copy-done | bytes 1048
  2.3 0.0 copy-start.2
  2.3 0.7 %copy-done.2 = s32[4,512]{1,0:T(4,128)S(1)} copy-done((s32[4,512]{1,0:T(4,128)S(1)}, s32[4,512]{1,0:T(4,128)}, u32[]{:S(2)}) %copy-start.2) | copy-done | bytes 8216
  3.0 0.0 copy-start.6
  3.0 0.7 %copy-done.6 = f32[512]{0:T(512)S(1)} copy-done((f32[512]{0:T(512)S(1)}, f32[512]{0:T(512)}, u32[]{:S(2)}) %copy-start.6) | copy-done | bytes 2072
  3.7 0.0 copy-start.7
  3.7 0.7 %copy-done.7 = f32[512]{0:T(512)S(1)} copy-done((f32[512]{0:T(512)S(1)}, f32[512]{0:T(512)}, u32[]{:S(2)}) %copy-start.7) | copy-done | bytes 2072
  4.4 0.0 copy-start.8
  4.4 0.7 %copy-done.8 = f32[1,4,64]{2,1,0:T(4,128)S(1)} copy-done((f32[1,4,64]{2,1,0:T(4,128)S(1)}, f32[1,4,64]{2,1,0:T(4,128)}, u32[]{:S(2)}) %copy-start.8) | copy-done | bytes 1048
  5.1 0.0 copy-start.9
  5.1 0.7 %copy-done.9 = f32[1,4,64]{2,1,0:T(4,128)S(1)} copy-done((f32[1,4,64]{2,1,0:T(4,128)S(1)}, f32[1,4,64]{2,1,0:T(4,128)}, u32[]{:S(2)}) %copy-start.9) | copy-done | bytes 1048
  5.7 29.0 %shard_map.100 = f32[256,128]{1,0:T(8,128)S(1)} custom-call(f32[256,128]{1,0:T(8,128)S(1)} %bitcast.6, f32[4,4,16]{2,1,0:T(4,128)S(1)} %copy-done.1, f32[4,4]{1,0:T(4,128)S(1)} %copy-done.3, s32[4,4]{1,0:T(4,128)S(1)} %copy-done.4, f32[1,512]{1,0:T(1,128)S(1)} %bitcast.7, f32[1,512]{1,0:T(1,128)S(1)} %bitcast.8, f32[1,512]{1,0:T(1,128)S(1)} %bitcast.9, ...), custom_call_target="tpu_custom_call" | custom-call | tf_op jit(solution)/shard_map/pallas_call | solution.py:568
  34.8 0.7 %copy.12 = f32[4,4,16,128]{3,2,1,0:T(8,128)} copy(f32[4,4,16,128]{3,2,1,0:T(8,128)S(1)} %bitcast.5) | data formatting | bytes 262144
Async XLA Ops:
  0.0 0.7 %copy-start.5 = (f32[512]{0:T(512)S(1)}, f32[512]{0:T(512)}, u32[]{:S(2)}) copy-start(f32[512]{0:T(512)} %param.14) | copy-start | bytes 6148
  0.0 0.7 %copy-start.4 = (s32[4,4]{1,0:T(4,128)S(1)}, s32[4,4]{1,0:T(4,128)}, u32[]{:S(2)}) copy-start(s32[4,4]{1,0:T(4,128)} %refs_3_.1) | copy-start | bytes 196
  0.0 0.7 %copy-start.3 = (f32[4,4]{1,0:T(4,128)S(1)}, f32[4,4]{1,0:T(4,128)}, u32[]{:S(2)}) copy-start(f32[4,4]{1,0:T(4,128)} %refs_2_.1) | copy-start | bytes 196
  0.7 0.9 %copy-start = (f32[4,4,16,128]{3,2,1,0:T(8,128)S(1)}, f32[4,4,16,128]{3,2,1,0:T(8,128)}, u32[]{:S(2)}) copy-start(f32[4,4,16,128]{3,2,1,0:T(8,128)} %param.10) | copy-start | bytes 393220
  1.6 0.7 %copy-start.1 = (f32[4,4,16]{2,1,0:T(4,128)S(1)}, f32[4,4,16]{2,1,0:T(4,128)}, u32[]{:S(2)}) copy-start(f32[4,4,16]{2,1,0:T(4,128)} %refs_1_.1) | copy-start | bytes 3076
  2.3 0.7 %copy-start.2 = (s32[4,512]{1,0:T(4,128)S(1)}, s32[4,512]{1,0:T(4,128)}, u32[]{:S(2)}) copy-start(s32[4,512]{1,0:T(4,128)} %refs_7_.1) | copy-start | bytes 24580
  3.0 0.7 %copy-start.6 = (f32[512]{0:T(512)S(1)}, f32[512]{0:T(512)}, u32[]{:S(2)}) copy-start(f32[512]{0:T(512)} %param.15) | copy-start | bytes 6148
  3.7 0.7 %copy-start.7 = (f32[512]{0:T(512)S(1)}, f32[512]{0:T(512)}, u32[]{:S(2)}) copy-start(f32[512]{0:T(512)} %param.16) | copy-start | bytes 6148
  4.4 0.7 %copy-start.8 = (f32[1,4,64]{2,1,0:T(4,128)S(1)}, f32[1,4,64]{2,1,0:T(4,128)}, u32[]{:S(2)}) copy-start(f32[1,4,64]{2,1,0:T(4,128)} %refs_8_.1) | copy-start | bytes 3076
  5.1 0.7 %copy-start.9 = (f32[1,4,64]{2,1,0:T(4,128)S(1)}, f32[1,4,64]{2,1,0:T(4,128)}, u32[]{:S(2)}) copy-start(f32[1,4,64]{2,1,0:T(4,128)} %refs_9_.1) | copy-start | bytes 3076
where the time goes:
time: 35.8 us; the launch traced here: 35.4 us
  Pallas kernels  29 us (81%)
  local copies, waits for them, and re-layouts  6.39 us (18%)
    pallas_call x1, Pallas kernels, react_and_advect(): pl.pallas_call(functools.partial(whole_kernel, bands, devices), out_shape...  29 us
    unnamed x21, local copies, waits for them, and re-layouts  6.39 us

commit v1 on v0

--- a/solution.py
+++ b/solution.py
@@ -582,7 +582,7 @@
             semaphores, semaphores, wind_semaphores, wind_semaphores, semaphores, semaphores,
         ],
         compiler_params=pltpu.CompilerParams(
-            collective_id=0, has_side_effects=True, vmem_limit_bytes=32 << 20
+            collective_id=0, has_side_effects=True, vmem_limit_bytes=67043328
         ),
     )(*operands)
 

time: 35.8 us -> 31.6 us (0.88)
  local copies, waits for them, and re-layouts: 6.39 us -> 1.57 us
  Pallas kernels: 29 us -> 29.8 us
    unnamed x21 -> x1, local copies, waits for them, and re-layouts: 6.39 us -> 1.57 us
    pallas_call x1, Pallas kernels: 29 us -> 29.8 us  [react_and_advect(): pl.pallas_call(functools.partial(whole_kernel, bands, devices), out_shape...]
where the time goes in v1:
time: 31.6 us; the launch traced here: 31.4 us
  Pallas kernels  29.8 us (94%)
  local copies, waits for them, and re-layouts  1.57 us (5%)
    pallas_call x1, Pallas kernels, react_and_advect(): pl.pallas_call(functools.partial(whole_kernel, bands, devices), out_shape...  29.8 us
    unnamed x1, local copies, waits for them, and re-layouts  1.57 us

profile of v1, /device:TPU:0, one launch (start us, length us, event | category | flops | bytes accessed | tf_op | source)
XLA Modules:
  0.0 31.4 jit_solution(5074302380949353257)
XLA Ops:
  0.0 29.8 %shard_map.100 = f32[256,128]{1,0:T(8,128)} custom-call(f32[256,128]{1,0:T(8,128)} %bitcast.6, f32[4,4,16]{2,1,0:T(4,128)} %refs_1_.1, f32[4,4]{1,0:T(4,128)} %refs_2_.1, s32[4,4]{1,0:T(4,128)} %refs_3_.1, f32[1,512]{1,0:T(1,128)} %bitcast.7, f32[1,512]{1,0:T(1,128)} %bitcast.8, f32[1,512]{1,0:T(1,128)} %bitcast.9, s32[4,512]{1,0:T(4,128)} %refs_7_.1, ...), custom_call_target="tpu_custom_call" | custom-call | tf_op jit(solution)/shard_map/pallas_call | solution.py:568
  29.9 1.6 %copy.12 = f32[4,4,16,128]{3,2,1,0:T(8,128)} copy(f32[4,4,16,128]{3,2,1,0:T(8,128)} %bitcast.5) | data formatting | bytes 262144
